TPU v7x, 128 devices: a whole 4x4x4 slice. The times are simulated.
128 devices in a mesh: dom: 16 (over x, y), cls: 8 (over z, core).
Axes of the slice: x: 4, y: 4, z: 4, core: 2. Of those that a mesh axis runs over, the one named last changes fastest.
Arguments:
- stack: bfloat16 [32768, 2, 64, 128], P(('dom', 'cls')), may hold values from -6 to 6
- batch_index: int32 [16384], P(('dom', 'cls')), may hold values from 0 to 255, as said below
- best_class: int32 [16384], P(('dom', 'cls')), may hold values from 0 to 511, as said below
- best_rot: int32 [16384], P(('dom', 'cls')), may hold values from 0 to 63
- best_shift: int32 [16384, 2], P(('dom', 'cls')), may hold values from -4 to 4
- ctf: bfloat16 [16384, 64], P(('dom', 'cls')), may hold values from -1 to 1
- averages: float32 [512, 2, 64, 128], P(('dom', 'cls')), may hold values from -6 to 6
- velocity: float32 [512, 2, 64, 128], P(('dom', 'cls')), may hold values from -3 to 3
Outputs:
- new_averages: float32 [512, 2, 64, 128], P(('dom', 'cls'))
- new_velocity: float32 [512, 2, 64, 128], P(('dom', 'cls'))
- errors: float32 [16384], P(('dom', 'cls'))
Inputs may be any that keep to these rules, and one draw needn't show every extreme that they name: `batch_index`: each aligned block of 128 entries (one device's particles) holds distinct row numbers into that device's own 256 rows of stack. `best_class`: classes c with equal c // 32 form a group. In each aligned block of 128 entries (one device's particles) at most 16 entries name classes of one group, and some group is named by exactly 16 entries of that block.
All inputs are finite; a program needn't handle non-finite values.
Results may differ from a plain program's by a relative error of at most 0.0026.
Values may be sent and summed in bfloat16 or wider, within the bound.
No kernel may reach another device: no remote copies, remote signals or barrier semaphores. Data moves between devices by JAX's collectives and lax.ppermute only.
A program may use at most 128 MiB of HBM per device.

v0:
```python
import jax
import jax.numpy as jnp
from jax import lax
from jax.sharding import PartitionSpec as P

IMG = 128
TWO_PI = 6.283185307179586
MOMENTUM = 0.9
RATE = 0.5
RIDGE = 1.0


def align_rows(rows, rotation, shift):
    cycles = rows.shape[2]
    angles = rows.shape[3]
    radius = jnp.arange(cycles).astype(jnp.float32) + 1.0
    theta = TWO_PI * jnp.arange(angles).astype(jnp.float32) / angles
    shift_x = shift[:, 0].astype(jnp.float32)
    shift_y = shift[:, 1].astype(jnp.float32)
    along = (
        jnp.cos(theta)[None, None, :] * shift_x[:, None, None]
        + jnp.sin(theta)[None, None, :] * shift_y[:, None, None]
    )
    phase = TWO_PI * radius[None, :, None] * along / IMG
    cosine = jnp.cos(phase)
    sine = jnp.sin(phase)
    real = rows[:, 0].astype(jnp.float32)
    imag = rows[:, 1].astype(jnp.float32)
    turned = jnp.stack([cosine * real - sine * imag, sine * real + cosine * imag], axis=1).astype(
        jnp.bfloat16
    )
    source = (jnp.arange(angles)[None, :] + 2 * rotation[:, None]) % angles
    permute = (source[:, :, None] == jnp.arange(angles)[None, None, :]).astype(jnp.bfloat16)
    moved = jnp.einsum("pskb,pab->pska", turned, permute, preferred_element_type=jnp.float32)
    return moved.astype(jnp.bfloat16)


def class_table(marker, column):
    local = marker.astype(jnp.int32) - 1
    return (jnp.arange(column)[:, None] == local[None, :]).astype(jnp.bfloat16)


def class_partials(table, terms, gamma):
    grads = jnp.dot(table, terms, preferred_element_type=jnp.float32)
    gamma_float = gamma.astype(jnp.float32)
    weights = jnp.dot(
        table.astype(jnp.float32),
        gamma_float * gamma_float,
        precision=lax.Precision.HIGHEST,
        preferred_element_type=jnp.float32,
    )
    return (grads, weights)


def on_device(stack, batch_index, best_class, best_rot, best_shift, ctf, averages, velocity):
    count = batch_index.shape[0]
    cycles = ctf.shape[1]
    angles = stack.shape[3]
    stored = stack.shape[0]
    flat = 2 * cycles * angles
    owners = lax.axis_size("dom")
    column = lax.axis_size("cls") * averages.shape[0]
    slots = 2 * count // owners
    buffer_rows = owners * slots
    picker = (batch_index[:, None] == jnp.arange(stored)[None, :]).astype(jnp.bfloat16)
    rows = jnp.dot(picker, stack.reshape(stored, flat), preferred_element_type=jnp.float32)
    rows = rows.astype(jnp.bfloat16).reshape(count, 2, cycles, angles)
    aligned = align_rows(rows, best_rot, best_shift)
    owner = best_class // column
    local_class = best_class - owner * column
    placed = (owner[:, None] == jnp.arange(owners)[None, :]).astype(jnp.int32)
    position = jnp.sum(jnp.cumsum(placed, axis=0) * placed, axis=1) - 1
    target = owner * slots + position
    dispatch = (jnp.arange(buffer_rows)[:, None] == target[None, :]).astype(jnp.bfloat16)

    def pack(payload):
        packed = jnp.dot(dispatch, payload, preferred_element_type=jnp.float32).astype(jnp.bfloat16)
        return packed.reshape(owners, slots, payload.shape[1])

    ctf_packed = pack(ctf)
    marker_packed = pack((local_class + 1).astype(jnp.bfloat16)[:, None]).reshape(owners, slots)
    every = lax.all_gather(averages.astype(jnp.bfloat16), ("dom", "cls"), axis=0, tiled=True)
    total_classes = every.shape[0]
    chooser = (best_class[:, None] == jnp.arange(total_classes)[None, :]).astype(jnp.bfloat16)
    model = jnp.dot(
        chooser, every.reshape(total_classes, flat), preferred_element_type=jnp.float32
    ).reshape(count, 2, cycles, angles)
    gamma_wide = ctf.astype(jnp.float32)[:, None, :, None]
    resid = aligned.astype(jnp.float32) - gamma_wide * model
    errors = jnp.mean(resid * resid, axis=(1, 2, 3))
    term = (gamma_wide * resid).astype(jnp.bfloat16).reshape(count, flat)
    arrived = (
        lax.all_to_all(pack(term), "dom", split_axis=0, concat_axis=0, tiled=True),
        lax.all_to_all(ctf_packed, "dom", split_axis=0, concat_axis=0, tiled=True),
        lax.all_to_all(marker_packed, "dom", split_axis=0, concat_axis=0, tiled=True),
    )
    got_terms = arrived[0].reshape(buffer_rows, flat)
    got_gamma = arrived[1].reshape(buffer_rows, cycles)
    table = class_table(arrived[2].reshape(buffer_rows), column)
    grads, weights = class_partials(table, got_terms, got_gamma)
    summed, weight_sum = (
        lax.psum_scatter(grads, "cls", scatter_dimension=0, tiled=True),
        lax.psum_scatter(weights, "cls", scatter_dimension=0, tiled=True),
    )
    step = (summed.reshape(averages.shape) - RIDGE * averages) / (
        weight_sum[:, None, :, None] + RIDGE
    )
    new_velocity = MOMENTUM * velocity + step
    new_averages = averages + RATE * new_velocity
    return (new_averages, new_velocity, errors)


def solution(mesh):
    in_specs = (
        P(("dom", "cls"), None, None, None),
        P(("dom", "cls")),
        P(("dom", "cls")),
        P(("dom", "cls")),
        P(("dom", "cls"), None),
        P(("dom", "cls"), None),
        P(("dom", "cls"), None, None, None),
        P(("dom", "cls"), None, None, None),
    )
    out_specs = (
        P(("dom", "cls"), None, None, None),
        P(("dom", "cls"), None, None, None),
        P(("dom", "cls")),
    )
    return jax.shard_map(
        on_device, mesh=mesh, in_specs=in_specs, out_specs=out_specs, check_vma=False
    )
```

profile of v0, /device:TPU:0, one launch (start us, length us, event | category | flops | bytes accessed | tf_op | source)
XLA Modules:
  0.0 396.0 jit_solution(6878493428379385242)
XLA Ops:
  7.2 0.0 all-gather.2.cloned.1.call-start
  7.2 1.6 convert_element_type.118
  8.8 0.0 all-gather.2.cloned.1.call-update
  8.9 0.7 and_select_fusion
  9.5 0.1 fusion.38
  9.6 0.2 reduce_window_sum.11
  9.8 0.2 select_reduce_fusion
  10.0 0.7 add_add_fusion
  10.6 0.8 fusion.30
  11.4 0.7 all_to_all.16
  12.2 7.1 %all-to-all-start = ((bf16[16,1,16]{2,1,0:T(2,128)(2,1)}), bf16[16,1,16]{2,1,0:T(2,128)(2,1)S(1)}, u32[]{:S(2)}, u32[]{:S(2)}) async-start(bf16[16,1,16]{2,1,0:T(2,128)(2,1)} %all_to_all.16), calls=%async_computation | async-start | bytes 16384 | tf_op jit(solution)/shard_map/all_to_all | solution.py:95
  19.3 0.8 copy.19
  20.1 8.8 %fusion.24 = bf16[16,8,128,128]{3,1,2,0:T(8,128)(2,1)S(1)} fusion(bf16[32,8,128,128]{3,2,1,0:T(8,128)(2,1)} %bitcast.59, s32[128]{0:T(128)} %param.9), kind=kOutput, calls=%fused_computation.30 | convolution fusion | flops 1075871744 | bytes 12583424 | tf_op jit(solution)/shard_map/dot_general | solution.py:66
  28.9 0.0 copy-start.5
  28.9 0.0 copy-start.3
  28.9 1.2 copy.27
  30.3 0.0 copy-done.5
  30.3 0.0 copy-done.3
  30.3 0.1 add_select_fusion
  30.4 0.1 multiply_add_fusion.1
  30.5 17.4 %fusion.8 = (bf16[128,1,64,128]{3,2,1,0:T(8,128)(2,1)S(1)}, bf16[128,1,64,128]{3,2,1,0:T(8,128)(2,1)}) fusion(f32[128,128]{1,0:T(8,128)S(1)} %multiply_add_fusion.1, f32[64]{0:T(128)S(1)} %add_multiply_fusion, bf16[128,2,64,128]{3,2,1,0:T(8,128)(2,1)S(1)} %bitcast.58), kind=kLoop, calls=%fused_computation.17 | loop fusion | flops 12582912 | bytes 8454400 | tf_op jit(solution)/shard_map/convert
  47.9 46.7 %all-gather.2.cloned.1.call-done = bf16[512,2,64,128]{3,2,1,0:T(8,128)(2,1)} async-done(((bf16[4,2,64,128]{3,2,1,0:T(8,128)(2,1)}), bf16[512,2,64,128]{3,2,1,0:T(8,128)(2,1)}) %all-gather.2.cloned.1.call-update) | async-done | bytes 16777232 | tf_op jit(solution)/shard_map/all_gather | solution.py:82
  94.6 23.9 %copy.25 = bf16[512,2,64,128]{0,3,2,1:T(8,128)(2,1)} copy(bf16[512,2,64,128]{3,2,1,0:T(8,128)(2,1)} %all-gather.2.cloned.1.call-done) | data formatting | bytes 33554432 | tf_op jit(solution)/shard_map/reshape | solution.py:86
  118.5 0.0 copy-done.4
  118.5 13.6 %fusion = f32[128,2,64,128]{0,3,2,1:T(8,128)} fusion(bf16[512,2,64,128]{0,3,2,1:T(8,128)(2,1)} %copy.25, s32[128]{0:T(128)S(1)} %copy-done.4), kind=kOutput, calls=%fused_computation.2 | convolution fusion | flops 2147549184 | bytes 25166336 | tf_op jit(solution)/shard_map/dot_general | solution.py:85
  132.1 8.7 %copy.21 = f32[128,2,64,128]{3,2,1,0:T(8,128)} copy(f32[128,2,64,128]{0,3,2,1:T(8,128)} %fusion) | data formatting | bytes 16777216 | tf_op jit(solution)/shard_map/dot_general | solution.py:85
  140.8 9.4 %multiply_reduce_fusion = (f32[128]{0:T(128)S(1)}, bf16[128,2,64,128]{3,2,1,0:T(8,128)(2,1)S(1)}) fusion(f32[128,2,64,128]{3,2,1,0:T(8,128)} %copy.21, f32[128,64]{1,0:T(8,128)S(1)} %copy.19, s32[128,128]{1,0:T(8,128)S(1)} %add_select_fusion, bf16[128,1,64,128]{3,2,1,0:T(8,128)(2,1)} %get-tuple-element.8, bf16[128,1,64,128]{3,2,1,0:T(8,128)(2,1)S(1)} %get-tuple-element.7), kind=kOutput, calls=%fused_computation.6 | convolution fusion | flops 557842304 | bytes 16876032 | tf_op jit(solution)/shard_map/pskb,pab->pska/dot_general | solution.py:34
  150.2 6.7 %convolution_convert_fusion = bf16[256,16384]{1,0:T(8,128)(2,1)} fusion(bf16[16,8,128,128]{3,2,1,0:T(8,128)(2,1)S(1)} %bitcast.60, s32[128]{0:T(128)S(1)} %add_add_fusion), kind=kOutput, calls=%fused_computation | convolution fusion | flops 1077968896 | bytes 12583424 | tf_op jit(solution)/shard_map/dot_general | solution.py:77
  156.9 0.0 all-to-all-done
  156.9 6.9 %all-to-all-start.1 = ((bf16[16,16,16384]{2,1,0:T(8,128)(2,1)}), bf16[16,16,16384]{2,1,0:T(8,128)(2,1)}, u32[]{:S(2)}, u32[]{:S(2)}) async-start(bf16[16,16,16384]{2,1,0:T(8,128)(2,1)} %bitcast.57), calls=%async_computation.1 | async-start | bytes 16777216 | tf_op jit(solution)/shard_map/all_to_all | solution.py:93
  163.8 0.0 all-reduce.4.cloned.1.call-start
  163.9 0.1 sub.32
  163.9 146.1 %all-to-all-done.1 = bf16[16,16,16384]{2,1,0:T(8,128)(2,1)} async-done(((bf16[16,16,16384]{2,1,0:T(8,128)(2,1)}), bf16[16,16,16384]{2,1,0:T(8,128)(2,1)}, u32[]{:S(2)}, u32[]{:S(2)}) %all-to-all-start.1) | async-done | bytes 8388640 | tf_op jit(solution)/shard_map/all_to_all | solution.py:93
  310.0 6.3 %fusion.41 = f32[32,16384]{1,0:T(8,128)} fusion(bf16[256,16384]{1,0:T(8,128)(2,1)} %bitcast.12, s32[256]{0:T(256)S(1)} %sub.32), kind=kOutput, calls=%fused_computation.59 | convolution fusion | flops 268443648 | bytes 10486784 | tf_op jit(solution)/shard_map/dot_general | solution.py:44
  316.3 0.0 all-reduce.4.cloned.1.call-update
  316.4 0.1 convolution_convert_fusion.2
  316.5 0.1 copy.22
  316.7 0.7 reshape.217
  317.4 11.7 %all-to-all-start.2 = ((bf16[16,2,512]{2,1,0:T(2,128)(2,1)}), bf16[16,2,512]{2,1,0:T(2,128)(2,1)S(1)}, u32[]{:S(2)}, u32[]{:S(2)}) async-start(bf16[16,2,512]{2,1,0:T(2,128)(2,1)} %reshape.217), calls=%async_computation.2 | async-start | bytes 65536 | tf_op jit(solution)/shard_map/all_to_all | solution.py:94
  329.1 0.6 dynamic-slice
  330.3 6.4 %all-to-all-done.2 = bf16[16,2,512]{2,1,0:T(2,128)(2,1)S(1)} async-done(((bf16[16,2,512]{2,1,0:T(2,128)(2,1)}), bf16[16,2,512]{2,1,0:T(2,128)(2,1)S(1)}, u32[]{:S(2)}, u32[]{:S(2)}) %all-to-all-start.2) | async-done | bytes 32800 | tf_op jit(solution)/shard_map/all_to_all | solution.py:94
  336.7 0.1 reshape.218
  336.8 0.2 fusion.40
  337.0 23.6 %all-reduce.1 = f32[32,64]{1,0:T(8,128)S(1)} all-reduce(f32[32,64]{1,0:T(8,128)S(1)} %fusion.40), channel_id=3, replica_groups=mesh['dom'=16,'cls'=8] {'cls'}, use_global_device_ids=true, to_apply=%region_3.4.clone | all-reduce | flops 2048 | bytes 16384
  360.6 0.5 broadcast_multiply_fusion
  361.1 26.0 %all-reduce.4.cloned.1.call-done = f32[32,16384]{1,0:T(8,128)} async-done(((f32[32,16384]{1,0:T(8,128)}), f32[32,16384]{1,0:T(8,128)}) %all-reduce.4.cloned.1.call-update) | async-done | bytes 2097168
  387.0 1.1 dynamic-slice_bitcast_fusion
  388.2 1.0 multiply_add_fusion
  (18 shorter events, 0.2 us)
Async XLA Ops:
  7.2 87.4 %all-gather.2.cloned.1.call-start = ((), (), s32[]{:S(2)}) async-start(), calls=%async_computation.3 | async-start | bytes 16908288 | tf_op jit(solution)/shard_map/all_gather | solution.py:82
  12.2 144.8 %all-to-all-start = ((bf16[16,1,16]{2,1,0:T(2,128)(2,1)}), bf16[16,1,16]{2,1,0:T(2,128)(2,1)S(1)}, u32[]{:S(2)}, u32[]{:S(2)}) async-start(bf16[16,1,16]{2,1,0:T(2,128)(2,1)} %all_to_all.16), calls=%async_computation | async-start | bytes 16384 | tf_op jit(solution)/shard_map/all_to_all | solution.py:95
  28.9 1.3 copy-start.5
  28.9 1.3 copy-start.3
  47.9 70.6 %copy-start.4 = (s32[128]{0:T(128)S(1)}, s32[128]{0:T(128)}, u32[]{:S(2)}) copy-start(s32[128]{0:T(128)} %param.10) | copy-start | bytes 1540
  156.9 153.1 %all-to-all-start.1 = ((bf16[16,16,16384]{2,1,0:T(8,128)(2,1)}), bf16[16,16,16384]{2,1,0:T(8,128)(2,1)}, u32[]{:S(2)}, u32[]{:S(2)}) async-start(bf16[16,16,16384]{2,1,0:T(8,128)(2,1)} %bitcast.57), calls=%async_computation.1 | async-start | bytes 16777216 | tf_op jit(solution)/shard_map/all_to_all | solution.py:93
  163.8 223.3 %all-reduce.4.cloned.1.call-start = ((), (), s32[]{:S(2)}) async-start(), calls=%async_computation.4 | async-start | bytes 4194304
  310.0 6.3 %copy-start.2 = (bf16[128,64]{0,1:T(8,128)(2,1)S(1)}, bf16[128,64]{0,1:T(8,128)(2,1)}, u32[]{:S(2)}) copy-start(bf16[128,64]{0,1:T(8,128)(2,1)} %param.13) | copy-start | bytes 49156
  310.0 19.1 %copy-start.6 = (u32[128]{0:T(128)S(1)}, u32[128]{0:T(128)}, u32[]{:S(2)}) copy-start(u32[128]{0:T(128)} %constant.71) | copy-start | bytes 1540
  310.0 78.1 %copy-start = (f32[4,2,64,128]{3,2,1,0:T(8,128)S(1)}, f32[4,2,64,128]{3,2,1,0:T(8,128)}, u32[]{:S(2)}) copy-start(f32[4,2,64,128]{3,2,1,0:T(8,128)} %param.14) | copy-start | bytes 786436
  310.0 78.1 %copy-start.1 = (f32[4,2,64,128]{3,2,1,0:T(8,128)S(1)}, f32[4,2,64,128]{3,2,1,0:T(8,128)}, u32[]{:S(2)}) copy-start(f32[4,2,64,128]{3,2,1,0:T(8,128)} %param.15) | copy-start | bytes 786436
  317.4 19.3 %all-to-all-start.2 = ((bf16[16,2,512]{2,1,0:T(2,128)(2,1)}), bf16[16,2,512]{2,1,0:T(2,128)(2,1)S(1)}, u32[]{:S(2)}, u32[]{:S(2)}) async-start(bf16[16,2,512]{2,1,0:T(2,128)(2,1)} %reshape.217), calls=%async_computation.2 | async-start | bytes 65536 | tf_op jit(solution)/shard_map/all_to_all | solution.py:94
Sparse Core Ops, SparseCore 0:
  11.7 82.8 all-gather.1
  316.5 70.5 all-reduce.3
where the time goes:
time: 397 us; the launch traced here: 396 us
  waiting for transfers between devices  225 us (57%)
  matrix products  45.9 us (12%)
  local copies, waits for them, and re-layouts  38.1 us (10%)
  starting transfers between devices  25.8 us (6%)
  blocking collectives  23.6 us (6%)
  other arithmetic  22.6 us (6%)
  between operations  14.9 us (4%)
    all_to_all x1, waiting for transfers between devices, on_device(): lax.all_to_all(pack(term), 'dom', split_axis=0, concat_axis=0, tiled=True)  146 us
    all_gather x1, waiting for transfers between devices, on_device(): lax.all_gather(averages.astype(jnp.bfloat16), ('dom', 'cls'), axis=0, til...  46.7 us
    unnamed x3, waiting for transfers between devices  26 us
    reshape x1, local copies, waits for them, and re-layouts, on_device(): every.reshape(total_classes, flat)  23.9 us
    unnamed x1, blocking collectives  23.6 us
    another operation x1, other arithmetic  17.4 us
    dot_general x1, matrix products, on_device(): jnp.dot(chooser, every.reshape(total_classes, flat), preferred_element_ty...  13.6 us
    all_to_all x1, starting transfers between devices, on_device(): lax.all_to_all(ctf_packed, 'dom', split_axis=0, concat_axis=0, tiled=True)  11.7 us
  transfers between devices with their start and end apart: 5, of which 4 were waited for; matrix products, arithmetic and copies ran while one was open for 24% of the time, Pallas kernels for 0%

commit v1 on v0

--- a/solution.py
+++ b/solution.py
@@ -8,6 +8,22 @@
 MOMENTUM = 0.9
 RATE = 0.5
 RIDGE = 1.0
+
+
+def swapped_with_each(value, axis, split, join):
+    ways, here = (lax.axis_size(axis), lax.axis_index(axis))
+    width = value.shape[split] // ways
+    shape = list(value.shape)
+    shape[split] = width
+    height = shape[join]
+    shape[join] = height * ways
+    full = jnp.zeros(shape, value.dtype)
+    for mask in range(ways):
+        part = lax.dynamic_slice_in_dim(value, (here ^ mask) * width, width, axis=split)
+        if mask:
+            part = lax.ppermute(part, axis, [(d, d ^ mask) for d in range(ways)])
+        full = lax.dynamic_update_slice_in_dim(full, part, (here ^ mask) * height, axis=join)
+    return full
 
 
 def align_rows(rows, rotation, shift):
@@ -90,7 +106,7 @@
     errors = jnp.mean(resid * resid, axis=(1, 2, 3))
     term = (gamma_wide * resid).astype(jnp.bfloat16).reshape(count, flat)
     arrived = (
-        lax.all_to_all(pack(term), "dom", split_axis=0, concat_axis=0, tiled=True),
+        swapped_with_each(pack(term), "dom", 0, 0),
         lax.all_to_all(ctf_packed, "dom", split_axis=0, concat_axis=0, tiled=True),
         lax.all_to_all(marker_packed, "dom", split_axis=0, concat_axis=0, tiled=True),
     )

time: 397 us -> 400 us (level)
  waiting for transfers between devices: 225 us -> 188 us
  local copies, waits for them, and re-layouts: 38.1 us -> 58.8 us
  blocking collectives: 23.6 us -> 38.4 us
  starting transfers between devices: 25.8 us -> 33.4 us
    all_to_all x2 -> x0, waiting for transfers between devices: 146 us -> none  [the longest x1 146 us: on_device(): lax.all_to_all(pack(term), 'dom', split_axis=0, concat_axis=0, tiled=True)]
    ppermute x0 -> x15, waiting for transfers between devices: none -> 102 us  [swapped_with_each(): part = lax.ppermute(part, axis, [(d, d ^ mask) for d in range(ways)])]
    ppermute x0 -> x15, starting transfers between devices: none -> 29.3 us  [swapped_with_each(): part = lax.ppermute(part, axis, [(d, d ^ mask) for d in range(ways)])]
    all_to_all x0 -> x1, blocking collectives: none -> 14.8 us  [on_device(): lax.all_to_all(marker_packed, 'dom', split_axis=0, concat_axis=0, tiled=T...]
    all_to_all x2 -> x0, starting transfers between devices: 14 us -> none  [the longest x1 7.12 us: on_device(): lax.all_to_all(marker_packed, 'dom', split_axis=0, concat_axis=0, tiled=T...]
    dynamic_update_slice x0 -> x15, local copies, waits for them, and re-layouts: none -> 12.6 us  [swapped_with_each(): lax.dynamic_update_slice_in_dim(full, part, (here ^ mask) * height, axis=...]
    all_to_all x1, starting transfers between devices: 11.7 us -> 4.02 us  [on_device(): lax.all_to_all(ctf_packed, 'dom', split_axis=0, concat_axis=0, tiled=True)]
    all_gather x1, waiting for transfers between devices: 46.7 us -> 52.6 us  [on_device(): lax.all_gather(averages.astype(jnp.bfloat16), ('dom', 'cls'), axis=0, til...]
  transfers between devices with their start and end apart: 5 -> 18, of which waited for: 4 -> 15; matrix products, arithmetic and copies ran while one was open for 24% -> 12% of each run, Pallas kernels for 0% -> 0%
where the time goes in v1:
time: 400 us; the launch traced here: 399 us
  waiting for transfers between devices  188 us (47%)
  local copies, waits for them, and re-layouts  58.8 us (15%)
  matrix products  42.2 us (11%)
  blocking collectives  38.4 us (10%)
  starting transfers between devices  33.4 us (8%)
  other arithmetic  23.2 us (6%)
  between operations  15 us (4%)
    ppermute x15, waiting for transfers between devices, swapped_with_each(): part = lax.ppermute(part, axis, [(d, d ^ mask) for d in range(ways)])  102 us
    all_gather x1, waiting for transfers between devices, on_device(): lax.all_gather(averages.astype(jnp.bfloat16), ('dom', 'cls'), axis=0, til...  52.6 us
    ppermute x15, starting transfers between devices, swapped_with_each(): part = lax.ppermute(part, axis, [(d, d ^ mask) for d in range(ways)])  29.3 us
    unnamed x3, waiting for transfers between devices  26.4 us
    reshape x1, local copies, waits for them, and re-layouts, on_device(): every.reshape(total_classes, flat)  23.9 us
    unnamed x1, blocking collectives  23.6 us
    another operation x1, other arithmetic  18.7 us
    all_to_all x1, blocking collectives, on_device(): lax.all_to_all(marker_packed, 'dom', split_axis=0, concat_axis=0, tiled=T...  14.8 us
  transfers between devices with their start and end apart: 18, of which 15 were waited for; matrix products, arithmetic and copies ran while one was open for 12% of the time, Pallas kernels for 0%

profile of v1, /device:TPU:0, one launch (start us, length us, event | category | flops | bytes accessed | tf_op | source)
XLA Modules:
  0.0 398.7 jit_solution(1124118968322734870)
XLA Ops:
  7.2 1.6 convert_element_type.118
  10.8 8.8 %fusion.24 = bf16[16,8,128,128]{3,1,2,0:T(8,128)(2,1)S(1)} fusion(bf16[32,8,128,128]{3,2,1,0:T(8,128)(2,1)} %bitcast.60, s32[128]{0:T(128)} %param.9), kind=kOutput, calls=%fused_computation.30 | convolution fusion | flops 1075871744 | bytes 12583424 | tf_op jit(solution)/shard_map/dot_general | solution.py:82
  19.6 3.2 copy.27
  23.3 18.7 %fusion.8 = (bf16[128,1,64,128]{3,2,1,0:T(8,128)(2,1)S(1)}, bf16[128,1,64,128]{3,2,1,0:T(8,128)(2,1)}) fusion(f32[128,128]{1,0:T(8,128)S(1)} %multiply_add_fusion.1, f32[64]{0:T(128)S(1)} %add_multiply_fusion, bf16[128,2,64,128]{3,2,1,0:T(8,128)(2,1)} %bitcast.59), kind=kLoop, calls=%fused_computation.17 | loop fusion | flops 12582912 | bytes 8454400 | tf_op jit(solution)/shard_map/convert
  42.0 52.6 %all-gather.2.cloned.1.call-done = bf16[512,2,64,128]{3,2,1,0:T(8,128)(2,1)} async-done(((bf16[4,2,64,128]{3,2,1,0:T(8,128)(2,1)}), bf16[512,2,64,128]{3,2,1,0:T(8,128)(2,1)}) %all-gather.2.cloned.1.call-update) | async-done | bytes 16777232 | tf_op jit(solution)/shard_map/all_gather | solution.py:98
  94.6 23.9 %copy.25 = bf16[512,2,64,128]{0,3,2,1:T(8,128)(2,1)} copy(bf16[512,2,64,128]{3,2,1,0:T(8,128)(2,1)} %all-gather.2.cloned.1.call-done) | data formatting | bytes 33554432 | tf_op jit(solution)/shard_map/reshape | solution.py:102
  118.5 13.6 %fusion = f32[128,2,64,128]{0,3,2,1:T(8,128)} fusion(bf16[512,2,64,128]{0,3,2,1:T(8,128)(2,1)} %copy.25, s32[128]{0:T(128)S(1)} %copy-done.5), kind=kOutput, calls=%fused_computation.2 | convolution fusion | flops 2147549184 | bytes 25166336 | tf_op jit(solution)/shard_map/dot_general | solution.py:101
  132.1 8.7 %copy.21 = f32[128,2,64,128]{3,2,1,0:T(8,128)} copy(f32[128,2,64,128]{0,3,2,1:T(8,128)} %fusion) | data formatting | bytes 16777216 | tf_op jit(solution)/shard_map/dot_general | solution.py:101
  140.8 9.6 %multiply_reduce_fusion = (f32[128]{0:T(128)S(1)}, bf16[128,2,64,128]{3,2,1,0:T(8,128)(2,1)S(1)}) fusion(f32[128,2,64,128]{3,2,1,0:T(8,128)} %copy.21, f32[128,64]{1,0:T(8,128)S(1)} %copy.19, s32[128,128]{1,0:T(8,128)S(1)} %add_select_fusion, bf16[128,1,64,128]{3,2,1,0:T(8,128)(2,1)} %get-tuple-element.24, bf16[128,1,64,128]{3,2,1,0:T(8,128)(2,1)S(1)} %get-tuple-element.23), kind=kOutput, calls=%fused_computation.6 | convolution fusion | flops 557842304 | bytes 16876032 | tf_op jit(solution)/shard_map/pskb,pab->pska/dot_general | solution.py:50
  150.5 3.5 convolution_convert_fusion
  153.9 0.9 broadcast_in_dim.2
  154.9 2.5 constant_dynamic-slice_fusion
  157.4 3.2 copy-done
  160.6 1.5 collective-permute-start
  162.3 14.8 %all_to_all.15 = bf16[16,1,16]{2,1,0:T(2,128)(2,1)S(1)} all-to-all(bf16[16,1,16]{2,1,0:T(2,128)(2,1)S(1)} %all_to_all.12), channel_id=1, replica_groups=mesh['dom'=16,'cls'=8] {'dom'}, dimensions={0} | all-to-all | bytes 1024 | tf_op jit(solution)/shard_map/all_to_all | solution.py:111
  177.2 0.9 collective-permute-start.1
  178.2 2.0 collective-permute-start.2
  180.2 1.5 collective-permute-start.3
  182.2 3.0 collective-permute-start.5
  186.1 7.0 %collective-permute-done.1 = bf16[1,16,16384]{2,1,0:T(8,128)(2,1)S(1)} collective-permute-done((bf16[1,16,16384]{2,1,0:T(8,128)(2,1)}, bf16[1,16,16384]{2,1,0:T(8,128)(2,1)S(1)}, u32[]{:S(2)}, u32[]{:S(2)}) %collective-permute-start.1) | collective-permute-done | bytes 524320 | tf_op jit(solution)/shard_map/ppermute | solution.py:24
  194.7 9.5 %collective-permute-done.2 = bf16[1,16,16384]{2,1,0:T(8,128)(2,1)S(1)} collective-permute-done((bf16[1,16,16384]{2,1,0:T(8,128)(2,1)}, bf16[1,16,16384]{2,1,0:T(8,128)(2,1)S(1)}, u32[]{:S(2)}, u32[]{:S(2)}) %collective-permute-start.2) | collective-permute-done | bytes 524320 | tf_op jit(solution)/shard_map/ppermute | solution.py:24
  204.2 3.0 collective-permute-start.7
  207.2 0.9 constant_dynamic-update-slice_fusion.11
  208.9 3.7 collective-permute-start.9
  213.4 4.4 %collective-permute-done.5 = bf16[1,16,16384]{2,1,0:T(8,128)(2,1)S(1)} collective-permute-done((bf16[1,16,16384]{2,1,0:T(8,128)(2,1)}, bf16[1,16,16384]{2,1,0:T(8,128)(2,1)S(1)}, u32[]{:S(2)}, u32[]{:S(2)}) %collective-permute-start.5) | collective-permute-done | bytes 524320 | tf_op jit(solution)/shard_map/ppermute | solution.py:24
  217.8 5.0 %collective-permute-start.10 = (bf16[1,16,16384]{2,1,0:T(8,128)(2,1)S(1)}, bf16[1,16,16384]{2,1,0:T(8,128)(2,1)S(1)}, u32[]{:S(2)}, u32[]{:S(2)}) collective-permute-start(bf16[1,16,16384]{2,1,0:T(8,128)(2,1)S(1)} %get-tuple-element.11), channel_id=1, source_target_pairs={{0,88},{8,80},{16,72},{24,64},{32,120},{40,112},{48,104},{56,96},{... | collective-permute-start | bytes 1572872 | tf_op jit(solution)/shard_map/ppermute | solution.py:24
  223.7 6.0 %collective-permute-done.6 = bf16[1,16,16384]{2,1,0:T(8,128)(2,1)S(1)} collective-permute-done((bf16[1,16,16384]{2,1,0:T(8,128)(2,1)}, bf16[1,16,16384]{2,1,0:T(8,128)(2,1)S(1)}, u32[]{:S(2)}, u32[]{:S(2)}) %collective-permute-start.6) | collective-permute-done | bytes 524320 | tf_op jit(solution)/shard_map/ppermute | solution.py:24
  229.6 2.7 collective-permute-start.11
  233.2 9.2 %collective-permute-done.7 = bf16[1,16,16384]{2,1,0:T(8,128)(2,1)S(1)} collective-permute-done((bf16[1,16,16384]{2,1,0:T(8,128)(2,1)}, bf16[1,16,16384]{2,1,0:T(8,128)(2,1)S(1)}, u32[]{:S(2)}, u32[]{:S(2)}) %collective-permute-start.7) | collective-permute-done | bytes 524320 | tf_op jit(solution)/shard_map/ppermute | solution.py:24
  242.4 1.4 collective-permute-start.12
  244.6 9.9 %collective-permute-done.8 = bf16[1,16,16384]{2,1,0:T(8,128)(2,1)S(1)} collective-permute-done((bf16[1,16,16384]{2,1,0:T(8,128)(2,1)}, bf16[1,16,16384]{2,1,0:T(8,128)(2,1)S(1)}, u32[]{:S(2)}, u32[]{:S(2)}) %collective-permute-start.8) | collective-permute-done | bytes 524320 | tf_op jit(solution)/shard_map/ppermute | solution.py:24
  254.5 1.3 collective-permute-start.13
  256.6 10.6 %collective-permute-done.9 = bf16[1,16,16384]{2,1,0:T(8,128)(2,1)S(1)} collective-permute-done((bf16[1,16,16384]{2,1,0:T(8,128)(2,1)}, bf16[1,16,16384]{2,1,0:T(8,128)(2,1)S(1)}, u32[]{:S(2)}, u32[]{:S(2)}) %collective-permute-start.9) | collective-permute-done | bytes 524320 | tf_op jit(solution)/shard_map/ppermute | solution.py:24
  267.2 2.0 collective-permute-start.14
  269.2 0.9 constant_dynamic-update-slice_fusion.4
  270.1 5.4 %collective-permute-done.10 = bf16[1,16,16384]{2,1,0:T(8,128)(2,1)S(1)} collective-permute-done((bf16[1,16,16384]{2,1,0:T(8,128)(2,1)S(1)}, bf16[1,16,16384]{2,1,0:T(8,128)(2,1)S(1)}, u32[]{:S(2)}, u32[]{:S(2)}) %collective-permute-start.10) | collective-permute-done | bytes 524320 | tf_op jit(solution)/shard_map/ppermute | solution.py:24
  276.3 8.7 %collective-permute-done.11 = bf16[1,16,16384]{2,1,0:T(8,128)(2,1)S(1)} collective-permute-done((bf16[1,16,16384]{2,1,0:T(8,128)(2,1)S(1)}, bf16[1,16,16384]{2,1,0:T(8,128)(2,1)S(1)}, u32[]{:S(2)}, u32[]{:S(2)}) %collective-permute-start.11) | collective-permute-done | bytes 524320 | tf_op jit(solution)/shard_map/ppermute | solution.py:24
  285.8 11.2 %collective-permute-done.12 = bf16[1,16,16384]{2,1,0:T(8,128)(2,1)S(1)} collective-permute-done((bf16[1,16,16384]{2,1,0:T(8,128)(2,1)S(1)}, bf16[1,16,16384]{2,1,0:T(8,128)(2,1)S(1)}, u32[]{:S(2)}, u32[]{:S(2)}) %collective-permute-start.12) | collective-permute-done | bytes 524320 | tf_op jit(solution)/shard_map/ppermute | solution.py:24
  297.9 11.9 %collective-permute-done.13 = bf16[1,16,16384]{2,1,0:T(8,128)(2,1)S(1)} collective-permute-done((bf16[1,16,16384]{2,1,0:T(8,128)(2,1)S(1)}, bf16[1,16,16384]{2,1,0:T(8,128)(2,1)S(1)}, u32[]{:S(2)}, u32[]{:S(2)}) %collective-permute-start.13) | collective-permute-done | bytes 524320 | tf_op jit(solution)/shard_map/ppermute | solution.py:24
  310.6 8.5 %collective-permute-done.14 = bf16[1,16,16384]{2,1,0:T(8,128)(2,1)S(1)} collective-permute-done((bf16[1,16,16384]{2,1,0:T(8,128)(2,1)S(1)}, bf16[1,16,16384]{2,1,0:T(8,128)(2,1)S(1)}, u32[]{:S(2)}, u32[]{:S(2)}) %collective-permute-start.14) | collective-permute-done | bytes 524320 | tf_op jit(solution)/shard_map/ppermute | solution.py:24
  319.1 0.9 constant_dynamic-update-slice_fusion.14
  320.0 6.3 %fusion.41 = f32[32,16384]{1,0:T(8,128)} fusion(bf16[256,16384]{1,0:T(8,128)(2,1)} %bitcast.58, s32[256]{0:T(256)S(1)} %sub.32), kind=kOutput, calls=%fused_computation.60 | convolution fusion | flops 268443648 | bytes 10486784 | tf_op jit(solution)/shard_map/dot_general | solution.py:60
  327.3 4.0 %all-to-all-start.1 = ((bf16[16,2,512]{2,1,0:T(2,128)(2,1)}), bf16[16,2,512]{2,1,0:T(2,128)(2,1)S(1)}, u32[]{:S(2)}, u32[]{:S(2)}) async-start(bf16[16,2,512]{2,1,0:T(2,128)(2,1)} %reshape.217), calls=%async_computation.1 | async-start | bytes 65536 | tf_op jit(solution)/shard_map/all_to_all | solution.py:110
  332.6 6.4 %all-to-all-done.1 = bf16[16,2,512]{2,1,0:T(2,128)(2,1)S(1)} async-done(((bf16[16,2,512]{2,1,0:T(2,128)(2,1)}), bf16[16,2,512]{2,1,0:T(2,128)(2,1)S(1)}, u32[]{:S(2)}, u32[]{:S(2)}) %all-to-all-start.1) | async-done | bytes 32800 | tf_op jit(solution)/shard_map/all_to_all | solution.py:110
  339.2 23.6 %all-reduce.1 = f32[32,64]{1,0:T(8,128)S(1)} all-reduce(f32[32,64]{1,0:T(8,128)S(1)} %fusion.40), channel_id=3, replica_groups=mesh['dom'=16,'cls'=8] {'cls'}, use_global_device_ids=true, to_apply=%region_3.4.clone | all-reduce | flops 2048 | bytes 16384
  363.3 26.4 %all-reduce.4.cloned.1.call-done = f32[32,16384]{1,0:T(8,128)} async-done(((f32[32,16384]{1,0:T(8,128)}), f32[32,16384]{1,0:T(8,128)}) %all-reduce.4.cloned.1.call-update) | async-done | bytes 2097168
  389.7 1.1 dynamic-slice_bitcast_fusion
  390.9 1.0 multiply_add_fusion
  (64 shorter events, 16.4 us)
Async XLA Ops:
  7.2 87.4 %all-gather.2.cloned.1.call-start = ((), (), s32[]{:S(2)}) async-start(), calls=%async_computation.2 | async-start | bytes 16908288 | tf_op jit(solution)/shard_map/all_gather | solution.py:98
  8.9 380.9 %all-reduce.4.cloned.1.call-start = ((), (), s32[]{:S(2)}) async-start(), calls=%async_computation.3 | async-start | bytes 4194304
  10.7 12.3 %copy-start.6 = (s32[128]{0:T(128)S(1)}, s32[128]{0:T(128)}, u32[]{:S(2)}) copy-start(s32[128]{0:T(128)} %param.11) | copy-start | bytes 1540
  10.7 12.3 %copy-start.5 = (s32[128]{0:T(128)S(1)}, s32[128]{0:T(128)}, u32[]{:S(2)}) copy-start(s32[128]{0:T(128)} %param.10) | copy-start | bytes 1540
  10.7 12.3 %copy-start.4 = (s32[128,2]{0,1:T(2,128)S(1)}, s32[128,2]{0,1:T(2,128)}, u32[]{:S(2)}) copy-start(s32[128,2]{0,1:T(2,128)} %param.12) | copy-start | bytes 3076
  157.4 3.2 copy-start
  160.6 21.6 %collective-permute-start = (bf16[1,16,16384]{2,1,0:T(8,128)(2,1)}, bf16[1,16,16384]{2,1,0:T(8,128)(2,1)S(1)}, u32[]{:S(2)}, u32[]{:S(2)}) collective-permute-start(bf16[1,16,16384]{2,1,0:T(8,128)(2,1)} %get-tuple-element.21), channel_id=1, source_target_pairs={{0,8},{8,0},{16,24},{24,16},{32,40},{40,32},{48,56},{56,48},{64,72... | collective-permute-start | bytes 1572872 | tf_op jit(solution)/shard_map/ppermute | solution.py:24
  177.2 15.8 %collective-permute-start.1 = (bf16[1,16,16384]{2,1,0:T(8,128)(2,1)}, bf16[1,16,16384]{2,1,0:T(8,128)(2,1)S(1)}, u32[]{:S(2)}, u32[]{:S(2)}) collective-permute-start(bf16[1,16,16384]{2,1,0:T(8,128)(2,1)} %get-tuple-element.20), channel_id=1, source_target_pairs={{0,16},{8,24},{16,0},{24,8},{32,48},{40,56},{48,32},{56,40},{64,80... | collective-permute-start | bytes 1572872 | tf_op jit(solution)/shard_map/ppermute | solution.py:24
  178.2 26.0 %collective-permute-start.2 = (bf16[1,16,16384]{2,1,0:T(8,128)(2,1)}, bf16[1,16,16384]{2,1,0:T(8,128)(2,1)S(1)}, u32[]{:S(2)}, u32[]{:S(2)}) collective-permute-start(bf16[1,16,16384]{2,1,0:T(8,128)(2,1)} %get-tuple-element.19), channel_id=1, source_target_pairs={{0,24},{8,16},{16,8},{24,0},{32,56},{40,48},{48,40},{56,32},{64,88... | collective-permute-start | bytes 1572872 | tf_op jit(solution)/shard_map/ppermute | solution.py:24
  180.2 27.9 %collective-permute-start.3 = (bf16[1,16,16384]{2,1,0:T(8,128)(2,1)}, bf16[1,16,16384]{2,1,0:T(8,128)(2,1)S(1)}, u32[]{:S(2)}, u32[]{:S(2)}) collective-permute-start(bf16[1,16,16384]{2,1,0:T(8,128)(2,1)} %get-tuple-element.18), channel_id=1, source_target_pairs={{0,32},{8,40},{16,48},{24,56},{32,0},{40,8},{48,16},{56,24},{64,96... | collective-permute-start | bytes 1572872 | tf_op jit(solution)/shard_map/ppermute | solution.py:24
  181.6 27.3 %collective-permute-start.4 = (bf16[1,16,16384]{2,1,0:T(8,128)(2,1)}, bf16[1,16,16384]{2,1,0:T(8,128)(2,1)S(1)}, u32[]{:S(2)}, u32[]{:S(2)}) collective-permute-start(bf16[1,16,16384]{2,1,0:T(8,128)(2,1)} %get-tuple-element.17), channel_id=1, source_target_pairs={{0,40},{8,32},{16,56},{24,48},{32,8},{40,0},{48,24},{56,16},{64,10... | collective-permute-start | bytes 1572872 | tf_op jit(solution)/shard_map/ppermute | solution.py:24
  182.2 35.6 %collective-permute-start.5 = (bf16[1,16,16384]{2,1,0:T(8,128)(2,1)}, bf16[1,16,16384]{2,1,0:T(8,128)(2,1)S(1)}, u32[]{:S(2)}, u32[]{:S(2)}) collective-permute-start(bf16[1,16,16384]{2,1,0:T(8,128)(2,1)} %get-tuple-element.16), channel_id=1, source_target_pairs={{0,48},{8,56},{16,32},{24,40},{32,16},{40,24},{48,0},{56,8},{64,11... | collective-permute-start | bytes 1572872 | tf_op jit(solution)/shard_map/ppermute | solution.py:24
  193.1 36.6 %collective-permute-start.6 = (bf16[1,16,16384]{2,1,0:T(8,128)(2,1)}, bf16[1,16,16384]{2,1,0:T(8,128)(2,1)S(1)}, u32[]{:S(2)}, u32[]{:S(2)}) collective-permute-start(bf16[1,16,16384]{2,1,0:T(8,128)(2,1)} %get-tuple-element.15), channel_id=1, source_target_pairs={{0,56},{8,48},{16,40},{24,32},{32,24},{40,16},{48,8},{56,0},{64,12... | collective-permute-start | bytes 1572872 | tf_op jit(solution)/shard_map/ppermute | solution.py:24
  204.2 38.2 %collective-permute-start.7 = (bf16[1,16,16384]{2,1,0:T(8,128)(2,1)}, bf16[1,16,16384]{2,1,0:T(8,128)(2,1)S(1)}, u32[]{:S(2)}, u32[]{:S(2)}) collective-permute-start(bf16[1,16,16384]{2,1,0:T(8,128)(2,1)} %get-tuple-element.14), channel_id=1, source_target_pairs={{0,64},{8,72},{16,80},{24,88},{32,96},{40,104},{48,112},{56,120},{... | collective-permute-start | bytes 1572872 | tf_op jit(solution)/shard_map/ppermute | solution.py:24
  208.1 46.4 %collective-permute-start.8 = (bf16[1,16,16384]{2,1,0:T(8,128)(2,1)}, bf16[1,16,16384]{2,1,0:T(8,128)(2,1)S(1)}, u32[]{:S(2)}, u32[]{:S(2)}) collective-permute-start(bf16[1,16,16384]{2,1,0:T(8,128)(2,1)} %get-tuple-element.13), channel_id=1, source_target_pairs={{0,72},{8,64},{16,88},{24,80},{32,104},{40,96},{48,120},{56,112},{... | collective-permute-start | bytes 1572872 | tf_op jit(solution)/shard_map/ppermute | solution.py:24
  208.9 58.3 %collective-permute-start.9 = (bf16[1,16,16384]{2,1,0:T(8,128)(2,1)}, bf16[1,16,16384]{2,1,0:T(8,128)(2,1)S(1)}, u32[]{:S(2)}, u32[]{:S(2)}) collective-permute-start(bf16[1,16,16384]{2,1,0:T(8,128)(2,1)} %get-tuple-element.12), channel_id=1, source_target_pairs={{0,80},{8,88},{16,64},{24,72},{32,112},{40,120},{48,96},{56,104},{... | collective-permute-start | bytes 1572872 | tf_op jit(solution)/shard_map/ppermute | solution.py:24
  217.8 57.6 %collective-permute-start.10 = (bf16[1,16,16384]{2,1,0:T(8,128)(2,1)S(1)}, bf16[1,16,16384]{2,1,0:T(8,128)(2,1)S(1)}, u32[]{:S(2)}, u32[]{:S(2)}) collective-permute-start(bf16[1,16,16384]{2,1,0:T(8,128)(2,1)S(1)} %get-tuple-element.11), channel_id=1, source_target_pairs={{0,88},{8,80},{16,72},{24,64},{32,120},{40,112},{48,104},{56,96},{... | collective-permute-start | bytes 1572872 | tf_op jit(solution)/shard_map/ppermute | solution.py:24
  229.6 55.3 %collective-permute-start.11 = (bf16[1,16,16384]{2,1,0:T(8,128)(2,1)S(1)}, bf16[1,16,16384]{2,1,0:T(8,128)(2,1)S(1)}, u32[]{:S(2)}, u32[]{:S(2)}) collective-permute-start(bf16[1,16,16384]{2,1,0:T(8,128)(2,1)S(1)} %get-tuple-element.10), channel_id=1, source_target_pairs={{0,96},{8,104},{16,112},{24,120},{32,64},{40,72},{48,80},{56,88},{... | collective-permute-start | bytes 1572872 | tf_op jit(solution)/shard_map/ppermute | solution.py:24
  242.4 54.6 %collective-permute-start.12 = (bf16[1,16,16384]{2,1,0:T(8,128)(2,1)S(1)}, bf16[1,16,16384]{2,1,0:T(8,128)(2,1)S(1)}, u32[]{:S(2)}, u32[]{:S(2)}) collective-permute-start(bf16[1,16,16384]{2,1,0:T(8,128)(2,1)S(1)} %get-tuple-element.9), channel_id=1, source_target_pairs={{0,104},{8,96},{16,120},{24,112},{32,72},{40,64},{48,88},{56,80},{... | collective-permute-start | bytes 1572872 | tf_op jit(solution)/shard_map/ppermute | solution.py:24
  254.5 55.3 %collective-permute-start.13 = (bf16[1,16,16384]{2,1,0:T(8,128)(2,1)S(1)}, bf16[1,16,16384]{2,1,0:T(8,128)(2,1)S(1)}, u32[]{:S(2)}, u32[]{:S(2)}) collective-permute-start(bf16[1,16,16384]{2,1,0:T(8,128)(2,1)S(1)} %get-tuple-element.8), channel_id=1, source_target_pairs={{0,112},{8,120},{16,96},{24,104},{32,80},{40,88},{48,64},{56,72},{... | collective-permute-start | bytes 1572872 | tf_op jit(solution)/shard_map/ppermute | solution.py:24
  267.2 51.9 %collective-permute-start.14 = (bf16[1,16,16384]{2,1,0:T(8,128)(2,1)S(1)}, bf16[1,16,16384]{2,1,0:T(8,128)(2,1)S(1)}, u32[]{:S(2)}, u32[]{:S(2)}) collective-permute-start(bf16[1,16,16384]{2,1,0:T(8,128)(2,1)S(1)} %get-tuple-element.7), channel_id=1, source_target_pairs={{0,120},{8,112},{16,104},{24,96},{32,88},{40,80},{48,72},{56,64},{... | collective-permute-start | bytes 1572872 | tf_op jit(solution)/shard_map/ppermute | solution.py:24
  276.3 50.0 %copy-start.3 = (bf16[128,64]{0,1:T(8,128)(2,1)S(1)}, bf16[128,64]{0,1:T(8,128)(2,1)}, u32[]{:S(2)}) copy-start(bf16[128,64]{0,1:T(8,128)(2,1)} %param.13) | copy-start | bytes 49156
  276.3 55.1 %copy-start.7 = (u32[128]{0:T(128)S(1)}, u32[128]{0:T(128)}, u32[]{:S(2)}) copy-start(u32[128]{0:T(128)} %constant.107) | copy-start | bytes 1540
  297.9 93.0 %copy-start.1 = (f32[4,2,64,128]{3,2,1,0:T(8,128)S(1)}, f32[4,2,64,128]{3,2,1,0:T(8,128)}, u32[]{:S(2)}) copy-start(f32[4,2,64,128]{3,2,1,0:T(8,128)} %param.14) | copy-start | bytes 786436
  297.9 93.0 %copy-start.2 = (f32[4,2,64,128]{3,2,1,0:T(8,128)S(1)}, f32[4,2,64,128]{3,2,1,0:T(8,128)}, u32[]{:S(2)}) copy-start(f32[4,2,64,128]{3,2,1,0:T(8,128)} %param.15) | copy-start | bytes 786436
  327.3 11.6 %all-to-all-start.1 = ((bf16[16,2,512]{2,1,0:T(2,128)(2,1)}), bf16[16,2,512]{2,1,0:T(2,128)(2,1)S(1)}, u32[]{:S(2)}, u32[]{:S(2)}) async-start(bf16[16,2,512]{2,1,0:T(2,128)(2,1)} %reshape.217), calls=%async_computation.1 | async-start | bytes 65536 | tf_op jit(solution)/shard_map/all_to_all | solution.py:110
Sparse Core Ops, SparseCore 0:
  11.7 82.8 all-gather.1
  326.4 63.2 all-reduce.3
